TPU v7x, 256 devices: a whole 4x4x8 slice. The times are simulated.
256 devices in a mesh: dp: 2 (over core), tile: 32 (over x, z), chan: 4 (over y).
Axes of the slice: x: 4, y: 4, z: 8, core: 2. Of those that a mesh axis runs over, the one named last changes fastest.
Arguments:
- pixels: float32 [48, 65536], P(None, ('dp', 'tile')), may hold values from -6 to 6
- tile_slide: int32 [1024], P(('dp', 'tile')), may hold values from 0 to 63, as said below
- tile_count: int32 [64], P(('dp', 'tile')), may hold values from 8 to 16, as said below
- w_patch: float32 [96, 48], P('chan'), may hold values from -0.875 to 0.875
- b_patch: float32 [96], P('chan'), may hold values from -3 to 3
- dw_kernel: float32 [96, 49], P('chan'), may hold values from -0.875 to 0.875
- dw_bias: float32 [96], P('chan'), may hold values from -3 to 3
- layernorm_gain: float32 [96], P('chan'), may hold values from 0.25 to 1.75
- layernorm_bias: float32 [96], P('chan'), may hold values from -3 to 3
- w_up: float32 [384, 96], P('chan'), may hold values from -0.625 to 0.625
- b_up: float32 [384], P('chan'), may hold values from -3 to 3
- w_down: float32 [384, 96], P('chan'), may hold values from -0.3125 to 0.3125
- b_down: float32 [96], P('chan'), may hold values from -3 to 3
- w_head: float32 [96], P('chan'), may hold values from -3 to 3
- target: float32 [128], P(('dp', 'tile')), may hold values from -4 to 4
Outputs:
- g_w_patch: float32 [96, 48], P('chan')
- g_b_patch: float32 [96], P('chan')
- g_dw_kernel: float32 [96, 49], P('chan')
- g_dw_bias: float32 [96], P('chan')
- g_ln_gain: float32 [96], P('chan')
- g_ln_bias: float32 [96], P('chan')
- g_w_up: float32 [384, 96], P('chan')
- g_b_up: float32 [384], P('chan')
- g_w_down: float32 [384, 96], P('chan')
- g_b_down: float32 [96], P('chan')
- g_w_head: float32 [96], P('chan')
- loss: float32 [], replicated
Inputs may be any that keep to these rules, and one draw needn't show every extreme that they name: `tile_slide`: in every slide group a run of 4 consecutive slides, neither the group's first nor its last, receives no slot; other slides may receive none too. `tile_count`: at least 8 live slots a device; some device has all 16 live in every draw.
All inputs are finite; a program needn't handle non-finite values.
Results may differ from a plain program's by a relative error of at most 0.00029.
Values sent between devices are 32-bit elements; how exact they have to be, the bound alone decides.
A program may use at most 64 MiB of HBM per device.

v0:
```python
import jax
import jax.numpy as jnp
from jax import lax
from jax.sharding import PartitionSpec as P

SIDE = 8
epsilon = 1e-06
highest = lax.Precision.HIGHEST


def depthwise(stem_grid, kernel, bias):
    side_len = stem_grid.shape[-1]
    padded = jnp.pad(stem_grid, ((0, 0), (0, 0), (3, 3), (3, 3)))
    total = jnp.zeros_like(stem_grid)
    for kernel_row in range(7):
        for kernel_col in range(7):
            weight_tap = kernel[:, kernel_row * 7 + kernel_col][:, None, None, None]
            total = (
                total
                + weight_tap
                * padded[
                    :, :, kernel_row : kernel_row + side_len, kernel_col : kernel_col + side_len
                ]
            )
    return total + bias[:, None, None, None]


def stem_local(w_patch, b_patch, dw_kernel, dw_bias, pixels):
    local_width = w_patch.shape[0]
    tile_num = pixels.shape[1] // (SIDE * SIDE)
    stem = jnp.dot(w_patch, pixels, precision=highest) + b_patch[:, None]
    mixed_features = depthwise(
        stem.reshape(local_width, tile_num, SIDE, SIDE), dw_kernel, dw_bias
    ).reshape(local_width, -1)
    return (stem, mixed_features)


def channel_pool(stem, layer_out, b_down, onehot, tile_num):
    local_width = stem.shape[0]
    features = stem + layer_out + b_down[:, None]
    pooled = jnp.mean(features.reshape(local_width, tile_num, SIDE * SIDE), axis=2)
    return jnp.dot(onehot.T, pooled.T, precision=highest)


def features_grad(onehot, d_sums_all, local_width, tile_num):
    area = SIDE * SIDE
    d_pooled = jnp.dot(onehot, d_sums_all, precision=highest).T
    return jnp.broadcast_to((d_pooled / area)[:, :, None], (local_width, tile_num, area)).reshape(
        local_width, tile_num * area
    )


def per_device(
    pixels,
    tile_slide,
    tile_count,
    w_patch,
    b_patch,
    dw_kernel,
    dw_bias,
    layernorm_gain,
    layernorm_bias,
    w_up,
    b_up,
    w_down,
    b_down,
    w_head,
    target,
):
    chan_count = lax.axis_size("chan")
    local_width = w_patch.shape[0]
    channel_width = local_width * chan_count
    tile_num = tile_slide.shape[0]
    slide_dev = target.shape[0]
    group_slides = slide_dev * lax.axis_size("tile")
    all_slides = group_slides * lax.axis_size("dp")
    live = (jnp.arange(tile_num, dtype=jnp.int32) < tile_count[0]).astype(jnp.float32)
    onehot = (tile_slide[:, None] == jnp.arange(group_slides, dtype=jnp.int32)[None, :]).astype(
        jnp.float32
    ) * live[:, None]
    slide_count = jnp.sum(onehot, axis=0)
    (stem, mixed_features), stem_pull = jax.vjp(
        lambda a, b, c, d: stem_local(a, b, c, d, pixels), w_patch, b_patch, dw_kernel, dw_bias
    )
    totals = lax.psum(
        (jnp.sum(mixed_features, axis=0), jnp.sum(mixed_features * mixed_features, axis=0)), "chan"
    )
    average_value = totals[0] / channel_width
    variance = totals[1] / channel_width - average_value * average_value
    inverse_deviation = lax.rsqrt(variance + epsilon)
    centered_input = (mixed_features - average_value) * inverse_deviation
    normalized_rows = centered_input * layernorm_gain[:, None] + layernorm_bias[:, None]
    normed_all = lax.all_gather(normalized_rows, "chan", axis=0, tiled=True)
    pre_act = jnp.dot(w_up, normed_all, precision=highest) + b_up[:, None]
    hidden, gelu_pull = jax.vjp(lambda value: jax.nn.gelu(value, approximate=False), pre_act)
    columns = w_down
    layer_out = lax.psum_scatter(
        jnp.dot(columns.T, hidden, precision=highest), "chan", scatter_dimension=0, tiled=True
    )
    slide_part = channel_pool(stem, layer_out, b_down, onehot, tile_num)
    owned_sums, owned_counts = (
        lax.psum_scatter(slide_part, "tile", scatter_dimension=0, tiled=True),
        lax.psum_scatter(slide_count, "tile", scatter_dimension=0, tiled=True),
    )
    counts = jnp.maximum(owned_counts, 1.0)
    slide_feat = owned_sums / counts[:, None]
    logit = lax.psum(jnp.dot(slide_feat, w_head, precision=highest), "chan")
    error = logit - target
    loss_part = 0.5 * jnp.sum(error * error) / all_slides
    d_logit = error / all_slides
    g_head = jnp.dot(slide_feat.T, d_logit, precision=highest)
    d_sums = d_logit[:, None] * w_head[None, :] / counts[:, None]
    d_sums_all = lax.all_gather(d_sums, "tile", axis=0, tiled=True)
    d_features = features_grad(onehot, d_sums_all, local_width, tile_num)
    g_b_down = jnp.sum(d_features, axis=1)
    d_out_all = lax.all_gather(d_features, "chan", axis=0, tiled=True)
    g_w_down = jnp.dot(hidden, d_out_all.T, precision=highest)
    d_hidden = jnp.dot(w_down, d_out_all, precision=highest)
    d_pre = gelu_pull(d_hidden)[0]
    g_w_up = jnp.dot(d_pre, normed_all.T, precision=highest)
    g_b_up = jnp.sum(d_pre, axis=1)
    columns = w_up
    normalized_gradient = lax.psum_scatter(
        jnp.dot(columns.T, d_pre, precision=highest), "chan", scatter_dimension=0, tiled=True
    )
    gain_gradient = jnp.sum(normalized_gradient * centered_input, axis=1)
    g_shift = jnp.sum(normalized_gradient, axis=1)
    centered_gradient = normalized_gradient * layernorm_gain[:, None]
    backward_sums = lax.psum(
        (jnp.sum(centered_gradient, axis=0), jnp.sum(centered_gradient * centered_input, axis=0)),
        "chan",
    )
    mixed_gradient = inverse_deviation * (
        centered_gradient
        - backward_sums[0] / channel_width
        - centered_input * (backward_sums[1] / channel_width)
    )
    g_patch, g_bpatch, g_kernel, g_dwbias = stem_pull((d_features, mixed_gradient))
    summed = lax.psum(
        (
            g_patch,
            g_bpatch,
            g_kernel,
            g_dwbias,
            gain_gradient,
            g_shift,
            g_w_up,
            g_b_up,
            g_w_down,
            g_b_down,
            g_head,
            loss_part,
        ),
        ("dp", "tile"),
    )
    return summed


def solution(mesh):
    in_specs = (
        P(None, ("dp", "tile")),
        P(("dp", "tile")),
        P(("dp", "tile")),
        P("chan", None),
        P("chan"),
        P("chan", None),
        P("chan"),
        P("chan"),
        P("chan"),
        P("chan", None),
        P("chan"),
        P("chan", None),
        P("chan"),
        P("chan"),
        P(("dp", "tile")),
    )
    out_specs = (
        P("chan", None),
        P("chan"),
        P("chan", None),
        P("chan"),
        P("chan"),
        P("chan"),
        P("chan", None),
        P("chan"),
        P("chan", None),
        P("chan"),
        P("chan"),
        P(),
    )
    return jax.shard_map(
        per_device, mesh=mesh, in_specs=in_specs, out_specs=out_specs, check_vma=False
    )
```

profile of v0, /device:TPU:1, one launch (start us, length us, event | category | flops | bytes accessed | tf_op | source)
XLA Modules:
  0.0 583.6 jit_solution(18157848405234515097)
XLA Ops:
  7.3 1.5 slice_reduce_fusion.46
  8.8 2.0 slice_reduce_fusion.48
  10.7 2.0 slice_reduce_fusion.47
  13.9 4.0 fusion.39
  18.3 9.6 %all-reduce.104 = (f32[1024]{0:T(1024)S(1)}, f32[1024]{0:T(1024)S(1)}) all-reduce(f32[1024]{0:T(1024)S(1)} %reduce_sum.554, f32[1024]{0:T(1024)S(1)} %reduce_sum.552), channel_id=1, replica_groups=mesh['dp'=2,'tile'=32,'chan'=4] {'chan'}, use_global_device_ids=true, to_apply=%region_3.4 | all-reduce | flops 2048 | bytes 16384 | tf_op jit(solution)/shard_map/psum | solution.py:85
  28.0 10.9 %all_gather.9 = f32[96,1024]{1,0:T(8,128)S(1)} all-gather(f32[24,1024]{1,0:T(8,128)S(1)} %multiply_add_fusion), channel_id=1, replica_groups=mesh['dp'=2,'tile'=32,'chan'=4] {'chan'}, dimensions={0}, use_global_device_ids=true | all-gather | bytes 491520 | tf_op jit(solution)/shard_map/all_gather | solution.py:93
  38.9 1.3 fusion
  40.3 1.3 convolution_bitcast_fusion.2
  43.6 24.4 %reduce-scatter.3.cloned.1.call-done = f32[24,1024]{1,0:T(8,128)} async-done(((f32[96,1024]{1,0:T(8,128)}), f32[24,1024]{1,0:T(8,128)}) %reduce-scatter.3.cloned.1.call-update) | async-done | bytes 98320 | tf_op jit(solution)/shard_map/reduce_scatter | solution.py:97
  69.6 115.5 %all-reduce.102 = (f32[64]{0:T(128)S(1)}, f32[64,24]{1,0:T(8,128)S(1)}) all-reduce(f32[64]{0:T(128)S(1)} %select_reduce_fusion, f32[64,24]{1,0:T(8,128)S(1)} %fusion.21), channel_id=4, replica_groups=mesh['dp'=2,'tile'=32,'chan'=4] {'tile'}, use_global_device_ids=true, to_apply=%region_8.9.clone | all-reduce | flops 1600 | bytes 12800
  185.4 7.3 %psum.121 = f32[2]{0:T(128)S(1)} all-reduce(f32[2]{0:T(128)S(1)} %convolution_bitcast_fusion.4), channel_id=1, replica_groups=mesh['dp'=2,'tile'=32,'chan'=4] {'chan'}, use_global_device_ids=true, to_apply=%region_9.10 | all-reduce | flops 2 | bytes 16 | tf_op jit(solution)/shard_map/psum | solution.py:107
  193.3 30.8 %all-gather = f32[32,2,24]{2,1,0:T(2,128)S(1)} all-gather(f32[1,2,24]{2,1,0:T(2,128)S(1)} %divide_bitcast_fusion), channel_id=1, replica_groups=mesh['dp'=2,'tile'=32,'chan'=4] {'tile'}, dimensions={0}, use_global_device_ids=true | all-gather | bytes 6336 | tf_op jit(solution)/shard_map/all_gather | solution.py:113
  224.6 9.9 %all_gather.11 = f32[96,1024]{1,0:T(8,128)S(1)} all-gather(f32[24,1024]{1,0:T(8,128)S(1)} %copy.43), channel_id=1, replica_groups=mesh['dp'=2,'tile'=32,'chan'=4] {'chan'}, dimensions={0}, use_global_device_ids=true | all-gather | bytes 491520 | tf_op jit(solution)/shard_map/all_gather | solution.py:116
  235.2 1.3 convolution_bitcast_fusion
  238.4 57.9 %reduce-scatter.5.cloned.1.call-done = f32[24,1024]{1,0:T(8,128)} async-done(((f32[96,1024]{1,0:T(8,128)}), f32[24,1024]{1,0:T(8,128)}) %reduce-scatter.5.cloned.1.call-update) | async-done | bytes 98320 | tf_op jit(solution)/shard_map/reduce_scatter | solution.py:123
  296.3 1.1 multiply_reduce_fusion.49
  297.4 7.4 %all-reduce.103 = (f32[1024]{0:T(1024)S(1)}, f32[1024]{0:T(1024)S(1)}) all-reduce(f32[1024]{0:T(1024)S(1)} %get-tuple-element.111, f32[1024]{0:T(1024)S(1)} %get-tuple-element.112), channel_id=1, replica_groups=mesh['dp'=2,'tile'=32,'chan'=4] {'chan'}, use_global_device_ids=true, to_apply=%region_14.15 | all-reduce | flops 2048 | bytes 16384 | tf_op jit(solution)/shard_map/psum | solution.py:129
  304.9 1.1 fusion.40
  307.0 1.5 multiply_reduce_fusion.46
  308.5 1.3 multiply_reduce_fusion.47
  310.7 1.2 broadcast_multiply_fusion.1
  312.0 1.2 broadcast_multiply_fusion
  313.2 5.1 pad_add_fusion
  319.8 256.4 %all-reduce.106 = (f32[24,48]{1,0:T(8,128)}, f32[24]{0:T(128)}, f32[24,49]{0,1:T(8,128)S(1)}, f32[24]{0:T(128)}, f32[24]{0:T(128)}, /*index=5*/f32[24]{0:T(128)}...) all-reduce(f32[24,48]{1,0:T(8,128)S(1)} %fusion.42, ...), channel_id=1, replica_groups=mesh['dp'=2,'tile'=32,'chan'=4] {'dp','tile'}, use_global_device_ids=true, to_apply=%region_15.16 | all-reduce | flops 21001 | bytes 168008 | tf_op jit(solution)/shard_map/psum | solution.py:139
  (63 shorter events, 11.3 us)
Async XLA Ops:
  7.2 5.5 copy-start
  7.2 20.7 %copy-start.3 = (f32[24]{0:T(128)S(1)}, f32[24]{0:T(128)}, u32[]{:S(2)}) copy-start(f32[24]{0:T(128)} %param.22) | copy-start | bytes 292
  7.2 20.7 %copy-start.4 = (f32[24]{0:T(128)S(1)}, f32[24]{0:T(128)}, u32[]{:S(2)}) copy-start(f32[24]{0:T(128)} %param.23) | copy-start | bytes 292
  7.2 60.8 %reduce-scatter.3.cloned.1.call-start = ((), (), s32[]{:S(2)}) async-start(), calls=%async_computation.2 | async-start | bytes 491520 | tf_op jit(solution)/shard_map/reduce_scatter | solution.py:97
  12.7 26.2 %copy-start.2 = (f32[96,96]{1,0:T(8,128)S(1)}, f32[96,96]{1,0:T(8,128)}, u32[]{:S(2)}) copy-start(f32[96,96]{1,0:T(8,128)} %param.24) | copy-start | bytes 110596
  12.7 26.2 %copy-start.8 = (f32[96]{0:T(128)S(1)}, f32[96]{0:T(128)}, u32[]{:S(2)}) copy-start(f32[96]{0:T(128)} %param.25) | copy-start | bytes 1156
  38.9 1.4 copy-start.1
  38.9 3.4 copy-start.10
  38.9 4.6 copy-start.9
  38.9 29.1 %copy-start.5 = (f32[24]{0:T(128)S(1)}, f32[24]{0:T(128)}, u32[]{:S(2)}) copy-start(f32[24]{0:T(128)} %param.27) | copy-start | bytes 292
  40.2 145.0 %copy-start.6 = (f32[24]{0:T(128)S(1)}, f32[24]{0:T(128)}, u32[]{:S(2)}) copy-start(f32[24]{0:T(128)} %param.28) | copy-start | bytes 292
  40.2 152.4 %copy-start.7 = (f32[2]{0:T(128)S(1)}, f32[2]{0:T(128)}, u32[]{:S(2)}) copy-start(f32[2]{0:T(128)} %param.29) | copy-start | bytes 28
  41.6 254.8 %reduce-scatter.5.cloned.1.call-start = ((), (), s32[]{:S(2)}) async-start(), calls=%async_computation.3 | async-start | bytes 491520 | tf_op jit(solution)/shard_map/reduce_scatter | solution.py:123
Sparse Core Ops, SparseCore 0:
  41.7 26.2 reduce-scatter.2
  236.6 59.6 reduce-scatter.4
where the time goes:
time: 584 us
  blocking collectives  448 us (77%)
  waiting for transfers between devices  82.3 us (14%)
  other arithmetic  21 us (4%)
  between operations  16.3 us (3%)
  matrix products  8.16 us (1%)
  local copies, waits for them, and re-layouts  7.87 us (1%)
    psum x1, blocking collectives, per_device(): lax.psum((g_patch, g_bpatch, g_kernel, g_dwbias, gain_gradient, g_shift,...  256 us
    unnamed x1, blocking collectives  116 us
    reduce_scatter x1, waiting for transfers between devices, per_device(): lax.psum_scatter(jnp.dot(columns.T, d_pre, precision=highest), 'chan', sc...  57.9 us
    all_gather x1, blocking collectives, per_device(): d_sums_all = lax.all_gather(d_sums, 'tile', axis=0, tiled=True)  30.8 us
    reduce_scatter x1, waiting for transfers between devices, per_device(): lax.psum_scatter(jnp.dot(columns.T, hidden, precision=highest), 'chan', s...  24.4 us
  transfers between devices with their start and end apart: 2, of which 2 were waited for; matrix products, arithmetic and copies ran while one was open for 0% of the time, Pallas kernels for 0%

commit v1 on v0

--- a/solution.py
+++ b/solution.py
@@ -6,6 +6,11 @@
 SIDE = 8
 epsilon = 1e-06
 highest = lax.Precision.HIGHEST
+
+
+def exchange_gather(value, mesh_axis, dim):
+    sent = jnp.stack([value] * lax.axis_size(mesh_axis))
+    return jnp.concatenate(lax.all_to_all(sent, mesh_axis, 0, 0), axis=dim)
 
 
 def depthwise(stem_grid, kernel, bias):
@@ -110,7 +115,7 @@
     d_logit = error / all_slides
     g_head = jnp.dot(slide_feat.T, d_logit, precision=highest)
     d_sums = d_logit[:, None] * w_head[None, :] / counts[:, None]
-    d_sums_all = lax.all_gather(d_sums, "tile", axis=0, tiled=True)
+    d_sums_all = exchange_gather(d_sums, "tile", 0)
     d_features = features_grad(onehot, d_sums_all, local_width, tile_num)
     g_b_down = jnp.sum(d_features, axis=1)
     d_out_all = lax.all_gather(d_features, "chan", axis=0, tiled=True)

time: 584 us -> 555 us (0.950)
  blocking collectives: 448 us -> 429 us
  waiting for transfers between devices: 82.3 us -> 72 us
    all_gather x1 -> x0, blocking collectives: 30.8 us -> none  [per_device(): d_sums_all = lax.all_gather(d_sums, 'tile', axis=0, tiled=True)]
    all_to_all x0 -> x1, blocking collectives: none -> 11.7 us  [exchange_gather(): return jnp.concatenate(lax.all_to_all(sent, mesh_axis, 0, 0), axis=dim)]
    reduce_scatter x1, waiting for transfers between devices: 57.9 us -> 47.6 us  [per_device(): lax.psum_scatter(jnp.dot(columns.T, d_pre, precision=highest), 'chan', sc...]
where the time goes in v1:
time: 555 us; the launch traced here: 554 us
  blocking collectives  429 us (77%)
  waiting for transfers between devices  72 us (13%)
  other arithmetic  21 us (4%)
  between operations  16.3 us (3%)
  matrix products  8.16 us (1%)
  local copies, waits for them, and re-layouts  7.88 us (1%)
    psum x1, blocking collectives, per_device(): lax.psum((g_patch, g_bpatch, g_kernel, g_dwbias, gain_gradient, g_shift,...  256 us
    unnamed x1, blocking collectives  116 us
    reduce_scatter x1, waiting for transfers between devices, per_device(): lax.psum_scatter(jnp.dot(columns.T, d_pre, precision=highest), 'chan', sc...  47.6 us
    reduce_scatter x1, waiting for transfers between devices, per_device(): lax.psum_scatter(jnp.dot(columns.T, hidden, precision=highest), 'chan', s...  24.4 us
    all_to_all x1, blocking collectives, exchange_gather(): return jnp.concatenate(lax.all_to_all(sent, mesh_axis, 0, 0), axis=dim)  11.7 us
  transfers between devices with their start and end apart: 2, of which 2 were waited for; matrix products, arithmetic and copies ran while one was open for 0% of the time, Pallas kernels for 0%

profile of v1, /device:TPU:1, one launch (start us, length us, event | category | flops | bytes accessed | tf_op | source)
XLA Modules:
  0.0 554.1 jit_solution(8955730366489301886)
XLA Ops:
  7.3 1.5 slice_reduce_fusion.46
  8.8 2.0 slice_reduce_fusion.48
  10.7 2.0 slice_reduce_fusion.47
  13.9 4.0 fusion.39
  18.3 9.6 %all-reduce.104 = (f32[1024]{0:T(1024)S(1)}, f32[1024]{0:T(1024)S(1)}) all-reduce(f32[1024]{0:T(1024)S(1)} %reduce_sum.554, f32[1024]{0:T(1024)S(1)} %reduce_sum.552), channel_id=1, replica_groups=mesh['dp'=2,'tile'=32,'chan'=4] {'chan'}, use_global_device_ids=true, to_apply=%region_3.4 | all-reduce | flops 2048 | bytes 16384 | tf_op jit(solution)/shard_map/psum | solution.py:90
  28.0 10.9 %all_gather.6 = f32[96,1024]{1,0:T(8,128)S(1)} all-gather(f32[24,1024]{1,0:T(8,128)S(1)} %multiply_add_fusion), channel_id=1, replica_groups=mesh['dp'=2,'tile'=32,'chan'=4] {'chan'}, dimensions={0}, use_global_device_ids=true | all-gather | bytes 491520 | tf_op jit(solution)/shard_map/all_gather | solution.py:98
  38.9 1.3 fusion
  40.3 1.3 convolution_bitcast_fusion.2
  43.6 24.4 %reduce-scatter.3.cloned.1.call-done = f32[24,1024]{1,0:T(8,128)} async-done(((f32[96,1024]{1,0:T(8,128)}), f32[24,1024]{1,0:T(8,128)}) %reduce-scatter.3.cloned.1.call-update) | async-done | bytes 98320 | tf_op jit(solution)/shard_map/reduce_scatter | solution.py:102
  69.6 115.5 %all-reduce.102 = (f32[64]{0:T(128)S(1)}, f32[64,24]{1,0:T(8,128)S(1)}) all-reduce(f32[64]{0:T(128)S(1)} %select_reduce_fusion, f32[64,24]{1,0:T(8,128)S(1)} %fusion.21), channel_id=4, replica_groups=mesh['dp'=2,'tile'=32,'chan'=4] {'tile'}, use_global_device_ids=true, to_apply=%region_8.9.clone | all-reduce | flops 1600 | bytes 12800
  185.4 7.3 %psum.121 = f32[2]{0:T(128)S(1)} all-reduce(f32[2]{0:T(128)S(1)} %convolution_bitcast_fusion.4), channel_id=1, replica_groups=mesh['dp'=2,'tile'=32,'chan'=4] {'chan'}, use_global_device_ids=true, to_apply=%region_9.10 | all-reduce | flops 2 | bytes 16 | tf_op jit(solution)/shard_map/psum | solution.py:112
  193.3 11.7 %all_to_all.5 = f32[32,2,24]{2,1,0:T(2,128)S(1)} all-to-all(f32[32,2,24]{2,1,0:T(2,128)S(1)} %stack.2), channel_id=1, replica_groups=mesh['dp'=2,'tile'=32,'chan'=4] {'tile'}, dimensions={0} | all-to-all | bytes 12288 | tf_op jit(solution)/shard_map/all_to_all | solution.py:13
  205.4 9.9 %all_gather.7 = f32[96,1024]{1,0:T(8,128)S(1)} all-gather(f32[24,1024]{1,0:T(8,128)S(1)} %copy.43), channel_id=1, replica_groups=mesh['dp'=2,'tile'=32,'chan'=4] {'chan'}, dimensions={0}, use_global_device_ids=true | all-gather | bytes 491520 | tf_op jit(solution)/shard_map/all_gather | solution.py:121
  216.0 1.3 convolution_bitcast_fusion
  219.2 47.6 %reduce-scatter.5.cloned.1.call-done = f32[24,1024]{1,0:T(8,128)} async-done(((f32[96,1024]{1,0:T(8,128)}), f32[24,1024]{1,0:T(8,128)}) %reduce-scatter.5.cloned.1.call-update) | async-done | bytes 98320 | tf_op jit(solution)/shard_map/reduce_scatter | solution.py:128
  266.8 1.1 multiply_reduce_fusion.49
  267.9 7.4 %all-reduce.103 = (f32[1024]{0:T(1024)S(1)}, f32[1024]{0:T(1024)S(1)}) all-reduce(f32[1024]{0:T(1024)S(1)} %get-tuple-element.111, f32[1024]{0:T(1024)S(1)} %get-tuple-element.112), channel_id=1, replica_groups=mesh['dp'=2,'tile'=32,'chan'=4] {'chan'}, use_global_device_ids=true, to_apply=%region_14.15 | all-reduce | flops 2048 | bytes 16384 | tf_op jit(solution)/shard_map/psum | solution.py:134
  275.4 1.1 fusion.40
  277.5 1.5 multiply_reduce_fusion.46
  279.0 1.3 multiply_reduce_fusion.47
  281.2 1.2 broadcast_multiply_fusion.1
  282.5 1.2 broadcast_multiply_fusion
  283.7 5.1 pad_add_fusion
  290.3 256.3 %all-reduce.106 = (f32[24,48]{1,0:T(8,128)}, f32[24]{0:T(128)}, f32[24,49]{0,1:T(8,128)S(1)}, f32[24]{0:T(128)}, f32[24]{0:T(128)}, /*index=5*/f32[24]{0:T(128)}...) all-reduce(f32[24,48]{1,0:T(8,128)S(1)} %fusion.42, ...), channel_id=1, replica_groups=mesh['dp'=2,'tile'=32,'chan'=4] {'dp','tile'}, use_global_device_ids=true, to_apply=%region_15.16 | all-reduce | flops 21001 | bytes 168008 | tf_op jit(solution)/shard_map/psum | solution.py:144
  (64 shorter events, 11.4 us)
Async XLA Ops:
  7.2 5.5 copy-start
  7.2 20.7 %copy-start.3 = (f32[24]{0:T(128)S(1)}, f32[24]{0:T(128)}, u32[]{:S(2)}) copy-start(f32[24]{0:T(128)} %param.22) | copy-start | bytes 292
  7.2 20.7 %copy-start.4 = (f32[24]{0:T(128)S(1)}, f32[24]{0:T(128)}, u32[]{:S(2)}) copy-start(f32[24]{0:T(128)} %param.23) | copy-start | bytes 292
  7.2 60.8 %reduce-scatter.3.cloned.1.call-start = ((), (), s32[]{:S(2)}) async-start(), calls=%async_computation.3 | async-start | bytes 491520 | tf_op jit(solution)/shard_map/reduce_scatter | solution.py:102
  12.7 26.2 %copy-start.2 = (f32[96,96]{1,0:T(8,128)S(1)}, f32[96,96]{1,0:T(8,128)}, u32[]{:S(2)}) copy-start(f32[96,96]{1,0:T(8,128)} %param.24) | copy-start | bytes 110596
  12.7 26.2 %copy-start.8 = (f32[96]{0:T(128)S(1)}, f32[96]{0:T(128)}, u32[]{:S(2)}) copy-start(f32[96]{0:T(128)} %param.25) | copy-start | bytes 1156
  38.9 1.4 copy-start.1
  38.9 3.4 copy-start.10
  38.9 4.6 copy-start.9
  38.9 29.1 %copy-start.5 = (f32[24]{0:T(128)S(1)}, f32[24]{0:T(128)}, u32[]{:S(2)}) copy-start(f32[24]{0:T(128)} %param.27) | copy-start | bytes 292
  40.2 145.0 %copy-start.6 = (f32[24]{0:T(128)S(1)}, f32[24]{0:T(128)}, u32[]{:S(2)}) copy-start(f32[24]{0:T(128)} %param.28) | copy-start | bytes 292
  40.2 152.4 %copy-start.7 = (f32[2]{0:T(128)S(1)}, f32[2]{0:T(128)}, u32[]{:S(2)}) copy-start(f32[2]{0:T(128)} %param.29) | copy-start | bytes 28
  41.6 225.3 %reduce-scatter.5.cloned.1.call-start = ((), (), s32[]{:S(2)}) async-start(), calls=%async_computation.4 | async-start | bytes 491520 | tf_op jit(solution)/shard_map/reduce_scatter | solution.py:128
Sparse Core Ops, SparseCore 0:
  41.7 26.2 reduce-scatter.2
  217.5 49.3 reduce-scatter.4
